TPU v7x, 512 devices: a whole 4x4x16 slice. The times are simulated.
512 devices in a mesh: swath: 32 (over z, core), chan: 16 (over x, y).
Axes of the slice: x: 4, y: 4, z: 16, core: 2. Of those that a mesh axis runs over, the one named last changes fastest.
Arguments:
- grid_profiles: bfloat16 [32768, 256], P('swath'), may hold values from -6 to 6
- send_lists: int32 [32, 32, 128], P('swath'), may hold values from 0 to 1023
- counts: int32 [32, 32], P('swath'), may hold values from 1 to 128, as said below
- angle_index: int32 [128], replicated, may hold values from 0 to 7
- jacobian: bfloat16 [3, 256, 608], P(None, None, 'chan'), may hold values from -0.375 to 0.375
- observed: bfloat16 [608, 131072], P('chan', 'swath'), may hold values from -6 to 6
- kappa: float32 [2, 608], P(None, 'chan'), may hold values from 0.04 to 0.24
- factor: bfloat16 [608, 608], P('chan')
Outputs:
- weighted: float32 [608, 131072], P('chan', 'swath')
Inputs may be any that keep to these rules, and one draw needn't show every extreme that they name: `counts`: some receiver gets 128 live slots from every sender; every entry is at least one.
All inputs are finite; a program needn't handle non-finite values.
Results may differ from a plain program's by a relative error of at most 0.0029.
Values may be sent and summed in bfloat16 or wider, within the bound.
A program may use at most 64 MiB of HBM per device.

v0:
```python
import math
import jax
import jax.numpy as jnp
from jax import lax
from jax.sharding import PartitionSpec as P

XTRACK = 128
NANG = 8
SWEEPS = 3
max_zenith = math.pi / 3.0


def edge_lines(block, width):
    count = lax.axis_size("swath")
    forward = [(i, i + 1) for i in range(count - 1)]
    backward = [(target, source) for source, target in forward]
    low = lax.ppermute(block[:, -width:], "swath", forward)
    high = lax.ppermute(block[:, :width], "swath", backward)
    return jnp.concatenate([low, block, high], axis=1)


def diffuse_once(extended, along_rate, cross_rate):
    center = extended[:, 1:-1]
    along_sum = extended[:, 2:] + extended[:, :-2] - 2.0 * center
    side_pad = jnp.pad(center, ((0, 0), (0, 0), (1, 1)))
    cross_sum = side_pad[:, :, 2:] + side_pad[:, :, :-2] - 2.0 * center
    return center + along_rate * along_sum + cross_rate * cross_sum


def on_device(grid_profiles, send_lists, counts, angle_index, jacobian, observed, kappa, factor):
    members = lax.axis_size("chan")
    member = lax.axis_index("chan")
    swaths = lax.axis_size("swath")
    swath = lax.axis_index("swath")
    slots = send_lists.shape[2]
    share = slots // members
    own_chan = observed.shape[0]
    pixel_count = observed.shape[1]
    line_count = pixel_count // XTRACK
    depth = grid_profiles.shape[1]
    rows = lax.dynamic_slice_in_dim(send_lists[0], member * share, share, axis=1)
    slot = member * share + jnp.arange(share, dtype=jnp.int32)
    live_slot = slot[None, :] < counts[0][:, None]
    zero_value = jnp.zeros((), grid_profiles.dtype)
    outgoing = jnp.where(live_slot[:, :, None], grid_profiles[rows], zero_value)
    incoming = lax.all_to_all(outgoing, "swath", split_axis=0, concat_axis=0, tiled=True)
    gathered = lax.all_gather(incoming, "chan", axis=0, tiled=False)
    pixel_profiles = gathered.transpose(1, 0, 2, 3).reshape(pixel_count, depth)
    whole_factor = lax.all_gather(factor, "chan", axis=0, tiled=True)
    model = jnp.einsum("mkc,pk->mcp", jacobian, pixel_profiles, preferred_element_type=jnp.float32)
    zenith = angle_index.astype(jnp.float32) * (max_zenith / (NANG - 1))
    slant_path = 1.0 / jnp.cos(zenith) - 1.0
    model = model.reshape(3, own_chan, line_count, XTRACK)
    departure = observed.astype(jnp.float32).reshape(own_chan, line_count, XTRACK) - (
        model[0] + slant_path * model[1] + slant_path * slant_path * model[2]
    )
    along_rate = kappa[0][:, None, None]
    cross_rate = kappa[1][:, None, None]
    field = edge_lines(departure, SWEEPS)
    line = swath * line_count - SWEEPS + jnp.arange(line_count + 2 * SWEEPS, dtype=jnp.int32)
    inside = (line >= 0) & (line < swaths * line_count)
    for sweep in range(SWEEPS):
        field = diffuse_once(field, along_rate, cross_rate)
        kept = inside[sweep + 1 : inside.shape[0] - sweep - 1]
        field = jnp.where(kept[None, :, None], field, 0.0)
    smoothed = field.reshape(own_chan, pixel_count).astype(jnp.bfloat16)
    every_channel = lax.all_to_all(smoothed, "chan", split_axis=1, concat_axis=0, tiled=True)
    weighted = jnp.dot(whole_factor, every_channel, preferred_element_type=jnp.float32)
    return lax.all_to_all(weighted, "chan", split_axis=0, concat_axis=1, tiled=True)


def solution(mesh):
    in_specs = (
        P("swath", None),
        P("swath", None, None),
        P("swath", None),
        P(),
        P(None, None, "chan"),
        P("chan", "swath"),
        P(None, "chan"),
        P("chan", None),
    )
    out_specs = P("chan", "swath")
    return jax.shard_map(
        on_device, mesh=mesh, in_specs=in_specs, out_specs=out_specs, check_vma=False
    )
```

profile of v0, /device:TPU:96, one launch (start us, length us, event | category | flops | bytes accessed | tf_op | source)
XLA Modules:
  0.0 163.9 jit_solution(3897559961001162474)
XLA Ops:
  6.5 0.0 copy-start
  6.5 0.0 all-gather.4.cloned.1.call-start
  6.5 0.9 compare_select_fusion
  7.4 0.1 reshape.103
  7.5 0.1 copy-done
  7.6 1.1 gather_fusion
  8.7 0.7 broadcast_compare_fusion
  9.5 0.1 bitcast_select_fusion
  9.6 28.5 %all_to_all.40 = bf16[32,8,256]{2,1,0:T(8,128)(2,1)} all-to-all(bf16[32,8,256]{2,1,0:T(8,128)(2,1)S(1)} %bitcast_select_fusion), channel_id=1, replica_groups=mesh['swath'=32,'chan'=16] {'swath'}, dimensions={0} | all-to-all | bytes 262144 | tf_op jit(solution)/shard_map/all_to_all | solution.py:46
  38.1 0.0 all-gather.4.cloned.1.call-update
  38.1 0.0 copy-done.1
  38.2 0.1 copy.18
  38.4 54.3 %all-gather.4.cloned.1.call-done = bf16[512,8,256]{2,1,0:T(8,128)(2,1)} async-done(((bf16[32,8,256]{2,1,0:T(8,128)(2,1)}), bf16[512,8,256]{2,1,0:T(8,128)(2,1)}) %all-gather.4.cloned.1.call-update) | async-done | bytes 2097168 | tf_op jit(solution)/shard_map/all_gather | solution.py:47
  92.7 1.8 %copy.15 = bf16[32,16,8,256]{3,2,1,0:T(8,128)(2,1)S(1)} copy(bf16[32,16,8,256]{3,2,0,1:T(8,128)(2,1)} %bitcast.57) | data formatting | bytes 4194304 | tf_op jit(solution)/shard_map/transpose | solution.py:48
  94.6 0.8 convolution_bitcast_fusion
  95.4 0.2 fusion.29
  95.6 0.1 copy.19
  95.7 0.1 copy.20
  95.9 0.1 copy.21
  96.0 0.3 fusion.23
  96.3 1.9 %collective-permute-start = (f32[38,3,128]{2,1,0:T(4,128)S(1)}, f32[38,3,128]{2,1,0:T(4,128)S(1)}, u32[]{:S(2)}, u32[]{:S(2)}) collective-permute-start(f32[38,3,128]{2,1,0:T(4,128)S(1)} %get-tuple-element.10), channel_id=1, source_target_pairs={{0,16},{16,32},{32,48},{48,64},{64,80},{80,96},{96,112},{112,128},... | collective-permute-start | bytes 175112 | tf_op jit(solution)/shard_map/ppermute | solution.py:17
  98.2 3.6 %collective-permute-start.1 = (f32[38,3,128]{2,1,0:T(4,128)S(1)}, f32[38,3,128]{2,1,0:T(4,128)S(1)}, u32[]{:S(2)}, u32[]{:S(2)}) collective-permute-start(f32[38,3,128]{2,1,0:T(4,128)S(1)} %get-tuple-element.11), channel_id=1, source_target_pairs={{16,0},{32,16},{48,32},{64,48},{80,64},{96,80},{112,96},{128,112},... | collective-permute-start | bytes 175112 | tf_op jit(solution)/shard_map/ppermute | solution.py:18
  101.9 0.1 slice.80
  102.0 0.1 slice.79
  102.1 0.1 slice.78
  102.1 0.0 collective-permute-done
  102.1 1.8 %collective-permute-done.1 = f32[38,3,128]{2,1,0:T(4,128)S(1)} collective-permute-done((f32[38,3,128]{2,1,0:T(4,128)S(1)}, f32[38,3,128]{2,1,0:T(4,128)S(1)}, u32[]{:S(2)}, u32[]{:S(2)}) %collective-permute-start.1) | collective-permute-done | bytes 58400 | tf_op jit(solution)/shard_map/ppermute | solution.py:18
  103.9 0.1 pad_maximum_fusion
  104.0 0.1 slice.110
  104.1 0.7 fusion.4
  104.8 0.1 slice.113
  104.8 0.7 fusion.9
  105.5 0.1 slice.116
  105.6 0.0 copy-start.3
  105.6 0.7 fusion.21
  106.3 0.1 convert_element_type.19
  106.4 0.8 copy.16
  107.2 4.9 %all-to-all-start.1 = ((bf16[38,16,256]{2,0,1:T(8,128)(2,1)}), bf16[38,16,256]{2,0,1:T(8,128)(2,1)S(1)}, u32[]{:S(2)}, u32[]{:S(2)}) async-start(bf16[38,16,256]{2,0,1:T(8,128)(2,1)} %copy.16), calls=%async_computation.1 | async-start | bytes 655360 | tf_op jit(solution)/shard_map/all_to_all | solution.py:67
  112.1 0.0 copy-done.3
  112.2 25.8 %all-gather.1 = bf16[16,38,608]{2,1,0:T(8,128)(2,1)S(1)} all-gather(bf16[1,38,608]{2,1,0:T(8,128)(2,1)S(1)} %bitcast.59), channel_id=1, replica_groups=mesh['swath'=32,'chan'=16] {'chan'}, dimensions={0}, use_global_device_ids=true | all-gather | bytes 785536 | tf_op jit(solution)/shard_map/all_gather | solution.py:49
  137.9 0.4 reshape.112
  138.3 0.0 all-to-all-done.1
  138.3 0.1 all_to_all.32
  138.4 0.4 convolution_bitcast_fusion.1
  138.8 0.1 all_to_all.33
  138.9 16.7 %all_to_all.41 = f32[16,38,256]{2,1,0:T(8,128)S(1)} all-to-all(f32[16,38,256]{2,1,0:T(8,128)S(1)} %all_to_all.33), channel_id=1, replica_groups=mesh['swath'=32,'chan'=16] {'chan'}, dimensions={0} | all-to-all | bytes 1245184 | tf_op jit(solution)/shard_map/all_to_all | solution.py:69
  155.6 0.2 copy.17
  155.9 1.2 copy.22
  (15 shorter events, 0.2 us)
Async XLA Ops:
  6.5 1.1 copy-start
  6.5 31.6 %copy-start.1 = (bf16[38,4096]{1,0:T(8,128)(2,1)S(1)}, bf16[38,4096]{1,0:T(8,128)(2,1)}, u32[]{:S(2)}) copy-start(bf16[38,4096]{1,0:T(8,128)(2,1)} %param.13) | copy-start | bytes 933892
  6.5 86.2 %all-gather.4.cloned.1.call-start = ((), (), s32[]{:S(2)}) async-start(), calls=%async_computation.3 | async-start | bytes 2228224 | tf_op jit(solution)/shard_map/all_gather | solution.py:47
  7.6 30.7 %copy-start.5 = (s32[128]{0:T(128)S(1)}, s32[128]{0:T(128)}, u32[]{:S(2)}) copy-start(s32[128]{0:T(128)} %param.11) | copy-start | bytes 1540
  7.6 30.8 %copy-start.4 = (f32[2,38]{1,0:T(2,128)S(1)}, f32[2,38]{1,0:T(2,128)}, u32[]{:S(2)}) copy-start(f32[2,38]{1,0:T(2,128)} %param.14) | copy-start | bytes 916
  92.7 1.9 %copy-start.2 = (bf16[3,256,38]{1,2,0:T(8,128)(2,1)S(1)}, bf16[3,256,38]{1,2,0:T(8,128)(2,1)}, u32[]{:S(2)}) copy-start(bf16[3,256,38]{1,2,0:T(8,128)(2,1)} %param.12) | copy-start | bytes 175108
  96.3 5.8 %collective-permute-start = (f32[38,3,128]{2,1,0:T(4,128)S(1)}, f32[38,3,128]{2,1,0:T(4,128)S(1)}, u32[]{:S(2)}, u32[]{:S(2)}) collective-permute-start(f32[38,3,128]{2,1,0:T(4,128)S(1)} %get-tuple-element.10), channel_id=1, source_target_pairs={{0,16},{16,32},{32,48},{48,64},{64,80},{80,96},{96,112},{112,128},... | collective-permute-start | bytes 175112 | tf_op jit(solution)/shard_map/ppermute | solution.py:17
  98.2 5.6 %collective-permute-start.1 = (f32[38,3,128]{2,1,0:T(4,128)S(1)}, f32[38,3,128]{2,1,0:T(4,128)S(1)}, u32[]{:S(2)}, u32[]{:S(2)}) collective-permute-start(f32[38,3,128]{2,1,0:T(4,128)S(1)} %get-tuple-element.11), channel_id=1, source_target_pairs={{16,0},{32,16},{48,32},{64,48},{80,64},{96,80},{112,96},{128,112},... | collective-permute-start | bytes 175112 | tf_op jit(solution)/shard_map/ppermute | solution.py:18
  105.6 6.5 %copy-start.3 = (bf16[38,608]{1,0:T(8,128)(2,1)S(1)}, bf16[38,608]{1,0:T(8,128)(2,1)}, u32[]{:S(2)}) copy-start(bf16[38,608]{1,0:T(8,128)(2,1)} %param.15) | copy-start | bytes 138628
  107.2 31.1 %all-to-all-start.1 = ((bf16[38,16,256]{2,0,1:T(8,128)(2,1)}), bf16[38,16,256]{2,0,1:T(8,128)(2,1)S(1)}, u32[]{:S(2)}, u32[]{:S(2)}) async-start(bf16[38,16,256]{2,0,1:T(8,128)(2,1)} %copy.16), calls=%async_computation.1 | async-start | bytes 655360 | tf_op jit(solution)/shard_map/all_to_all | solution.py:67
Sparse Core Ops, SparseCore 0:
  38.2 54.4 all-gather.3
where the time goes:
time: 164 us
  blocking collectives  71 us (43%)
  waiting for transfers between devices  56.1 us (34%)
  between operations  13.7 us (8%)
  starting transfers between devices  10.5 us (6%)
  local copies, waits for them, and re-layouts  7.18 us (4%)
  other arithmetic  4.24 us (3%)
    all_gather x1, waiting for transfers between devices, on_device(): gathered = lax.all_gather(incoming, 'chan', axis=0, tiled=False)  54.3 us
    all_to_all x1, blocking collectives, on_device(): lax.all_to_all(outgoing, 'swath', split_axis=0, concat_axis=0, tiled=True)  28.5 us
    all_gather x1, blocking collectives, on_device(): whole_factor = lax.all_gather(factor, 'chan', axis=0, tiled=True)  25.8 us
    all_to_all x1, blocking collectives, on_device(): lax.all_to_all(weighted, 'chan', split_axis=0, concat_axis=1, tiled=True)  16.7 us
    all_to_all x1, starting transfers between devices, on_device(): lax.all_to_all(smoothed, 'chan', split_axis=1, concat_axis=0, tiled=True)  4.94 us
    ppermute x1, starting transfers between devices, edge_lines(): high = lax.ppermute(block[:, :width], 'swath', backward)  3.64 us
  transfers between devices with their start and end apart: 4, of which 2 were waited for; matrix products, arithmetic and copies ran while one was open for 0% of the time, Pallas kernels for 0%

commit v1 on v0

--- a/solution.py
+++ b/solution.py
@@ -66,7 +66,10 @@
     smoothed = field.reshape(own_chan, pixel_count).astype(jnp.bfloat16)
     every_channel = lax.all_to_all(smoothed, "chan", split_axis=1, concat_axis=0, tiled=True)
     weighted = jnp.dot(whole_factor, every_channel, preferred_element_type=jnp.float32)
-    return lax.all_to_all(weighted, "chan", split_axis=0, concat_axis=1, tiled=True)
+    return jnp.concatenate(
+        lax.all_to_all(jnp.stack(jnp.split(weighted, lax.axis_size("chan"), axis=0)), "chan", 0, 0),
+        axis=1,
+    )
 
 
 def solution(mesh):

time: 164 us -> 164 us (level)
  no operation moved by 1% of the time
where the time goes in v1:
time: 164 us
  blocking collectives  71 us (43%)
  waiting for transfers between devices  56.1 us (34%)
  between operations  13.8 us (8%)
  starting transfers between devices  10.5 us (6%)
  local copies, waits for them, and re-layouts  7.21 us (4%)
  other arithmetic  4.24 us (3%)
    all_gather x1, waiting for transfers between devices, on_device(): gathered = lax.all_gather(incoming, 'chan', axis=0, tiled=False)  54.3 us
    all_to_all x1, blocking collectives, on_device(): lax.all_to_all(outgoing, 'swath', split_axis=0, concat_axis=0, tiled=True)  28.5 us
    all_gather x1, blocking collectives, on_device(): whole_factor = lax.all_gather(factor, 'chan', axis=0, tiled=True)  25.8 us
    all_to_all x1, blocking collectives, on_device(): lax.all_to_all(jnp.stack(jnp.split(weighted, lax.axis_size('chan'), axis=...  16.7 us
    all_to_all x1, starting transfers between devices, on_device(): lax.all_to_all(smoothed, 'chan', split_axis=1, concat_axis=0, tiled=True)  4.94 us
    ppermute x1, starting transfers between devices, edge_lines(): high = lax.ppermute(block[:, :width], 'swath', backward)  3.64 us
  transfers between devices with their start and end apart: 4, of which 2 were waited for; matrix products, arithmetic and copies ran while one was open for 0% of the time, Pallas kernels for 0%

profile of v1, /device:TPU:96, one launch (start us, length us, event | category | flops | bytes accessed | tf_op | source)
XLA Modules:
  0.0 164.1 jit_solution(5391022183880514071)
XLA Ops:
  6.5 0.0 copy-start
  6.5 0.0 all-gather.4.cloned.1.call-start
  6.5 0.9 compare_select_fusion
  7.4 0.1 reshape.108
  7.5 0.1 copy-done
  7.6 1.1 gather_fusion
  8.7 0.7 broadcast_compare_fusion
  9.5 0.1 bitcast_select_fusion
  9.6 28.5 %all_to_all.26 = bf16[32,8,256]{2,1,0:T(8,128)(2,1)} all-to-all(bf16[32,8,256]{2,1,0:T(8,128)(2,1)S(1)} %bitcast_select_fusion), channel_id=1, replica_groups=mesh['swath'=32,'chan'=16] {'swath'}, dimensions={0} | all-to-all | bytes 262144 | tf_op jit(solution)/shard_map/all_to_all | solution.py:46
  38.1 0.0 all-gather.4.cloned.1.call-update
  38.1 0.0 copy-done.1
  38.2 0.1 copy.15
  38.3 0.0 copy-done.5
  38.4 54.3 %all-gather.4.cloned.1.call-done = bf16[512,8,256]{2,1,0:T(8,128)(2,1)} async-done(((bf16[32,8,256]{2,1,0:T(8,128)(2,1)}), bf16[512,8,256]{2,1,0:T(8,128)(2,1)}) %all-gather.4.cloned.1.call-update) | async-done | bytes 2097168 | tf_op jit(solution)/shard_map/all_gather | solution.py:47
  92.7 1.8 %copy.12 = bf16[32,16,8,256]{3,2,1,0:T(8,128)(2,1)S(1)} copy(bf16[32,16,8,256]{3,2,0,1:T(8,128)(2,1)} %bitcast.121) | data formatting | bytes 4194304 | tf_op jit(solution)/shard_map/transpose | solution.py:48
  94.6 0.8 convolution_bitcast_fusion
  95.4 0.2 fusion.45
  95.6 0.1 copy.16
  95.7 0.1 copy.17
  95.9 0.1 copy.18
  96.0 0.3 fusion.23
  96.3 1.9 %collective-permute-start = (f32[38,3,128]{2,1,0:T(4,128)S(1)}, f32[38,3,128]{2,1,0:T(4,128)S(1)}, u32[]{:S(2)}, u32[]{:S(2)}) collective-permute-start(f32[38,3,128]{2,1,0:T(4,128)S(1)} %get-tuple-element.10), channel_id=1, source_target_pairs={{0,16},{16,32},{32,48},{48,64},{64,80},{80,96},{96,112},{112,128},... | collective-permute-start | bytes 175112 | tf_op jit(solution)/shard_map/ppermute | solution.py:17
  98.2 3.6 %collective-permute-start.1 = (f32[38,3,128]{2,1,0:T(4,128)S(1)}, f32[38,3,128]{2,1,0:T(4,128)S(1)}, u32[]{:S(2)}, u32[]{:S(2)}) collective-permute-start(f32[38,3,128]{2,1,0:T(4,128)S(1)} %get-tuple-element.11), channel_id=1, source_target_pairs={{16,0},{32,16},{48,32},{64,48},{80,64},{96,80},{112,96},{128,112},... | collective-permute-start | bytes 175112 | tf_op jit(solution)/shard_map/ppermute | solution.py:18
  101.9 0.1 slice.80
  102.0 0.1 slice.79
  102.1 0.1 slice.78
  102.1 0.0 collective-permute-done
  102.1 1.8 %collective-permute-done.1 = f32[38,3,128]{2,1,0:T(4,128)S(1)} collective-permute-done((f32[38,3,128]{2,1,0:T(4,128)S(1)}, f32[38,3,128]{2,1,0:T(4,128)S(1)}, u32[]{:S(2)}, u32[]{:S(2)}) %collective-permute-start.1) | collective-permute-done | bytes 58400 | tf_op jit(solution)/shard_map/ppermute | solution.py:18
  103.9 0.1 pad_maximum_fusion
  104.0 0.1 slice.110
  104.1 0.7 fusion.4
  104.8 0.1 slice.113
  104.8 0.7 fusion.9
  105.5 0.1 slice.116
  105.6 0.0 copy-start.3
  105.6 0.7 fusion.21
  106.3 0.1 convert_element_type.19
  106.4 0.8 copy.13
  107.2 4.9 %all-to-all-start.1 = ((bf16[38,16,256]{2,0,1:T(8,128)(2,1)}), bf16[38,16,256]{2,0,1:T(8,128)(2,1)S(1)}, u32[]{:S(2)}, u32[]{:S(2)}) async-start(bf16[38,16,256]{2,0,1:T(8,128)(2,1)} %copy.13), calls=%async_computation.1 | async-start | bytes 655360 | tf_op jit(solution)/shard_map/all_to_all | solution.py:67
  112.1 0.0 copy-done.3
  112.2 25.8 %all-gather.1 = bf16[16,38,608]{2,1,0:T(8,128)(2,1)S(1)} all-gather(bf16[1,38,608]{2,1,0:T(8,128)(2,1)S(1)} %bitcast.123), channel_id=1, replica_groups=mesh['swath'=32,'chan'=16] {'chan'}, dimensions={0}, use_global_device_ids=true | all-gather | bytes 785536 | tf_op jit(solution)/shard_map/all_gather | solution.py:49
  137.9 0.4 reshape.117
  138.3 0.0 all-to-all-done.1
  138.3 0.1 all_to_all.21
  138.4 0.4 convolution_bitcast_fusion.1
  139.1 16.7 %all_to_all.27 = f32[16,38,256]{2,1,0:T(8,128)S(1)} all-to-all(f32[16,38,256]{2,1,0:T(8,128)S(1)} %fusion.28), channel_id=1, replica_groups=mesh['swath'=32,'chan'=16] {'chan'}, dimensions={0} | all-to-all | bytes 1245184 | tf_op jit(solution)/shard_map/all_to_all | solution.py:70
  155.8 0.2 copy.14
  156.0 1.2 copy.19
  (30 shorter events, 0.3 us)
Async XLA Ops:
  6.5 1.1 copy-start
  6.5 31.6 %copy-start.1 = (bf16[38,4096]{1,0:T(8,128)(2,1)S(1)}, bf16[38,4096]{1,0:T(8,128)(2,1)}, u32[]{:S(2)}) copy-start(bf16[38,4096]{1,0:T(8,128)(2,1)} %param.13) | copy-start | bytes 933892
  6.5 86.2 %all-gather.4.cloned.1.call-start = ((), (), s32[]{:S(2)}) async-start(), calls=%async_computation.3 | async-start | bytes 2228224 | tf_op jit(solution)/shard_map/all_gather | solution.py:47
  7.6 30.7 %copy-start.5 = (s32[128]{0:T(128)S(1)}, s32[128]{0:T(128)}, u32[]{:S(2)}) copy-start(s32[128]{0:T(128)} %param.11) | copy-start | bytes 1540
  7.6 30.8 %copy-start.4 = (f32[2,38]{1,0:T(2,128)S(1)}, f32[2,38]{1,0:T(2,128)}, u32[]{:S(2)}) copy-start(f32[2,38]{1,0:T(2,128)} %param.14) | copy-start | bytes 916
  92.7 1.9 %copy-start.2 = (bf16[3,256,38]{1,2,0:T(8,128)(2,1)S(1)}, bf16[3,256,38]{1,2,0:T(8,128)(2,1)}, u32[]{:S(2)}) copy-start(bf16[3,256,38]{1,2,0:T(8,128)(2,1)} %param.12) | copy-start | bytes 175108
  96.3 5.8 %collective-permute-start = (f32[38,3,128]{2,1,0:T(4,128)S(1)}, f32[38,3,128]{2,1,0:T(4,128)S(1)}, u32[]{:S(2)}, u32[]{:S(2)}) collective-permute-start(f32[38,3,128]{2,1,0:T(4,128)S(1)} %get-tuple-element.10), channel_id=1, source_target_pairs={{0,16},{16,32},{32,48},{48,64},{64,80},{80,96},{96,112},{112,128},... | collective-permute-start | bytes 175112 | tf_op jit(solution)/shard_map/ppermute | solution.py:17
  98.2 5.6 %collective-permute-start.1 = (f32[38,3,128]{2,1,0:T(4,128)S(1)}, f32[38,3,128]{2,1,0:T(4,128)S(1)}, u32[]{:S(2)}, u32[]{:S(2)}) collective-permute-start(f32[38,3,128]{2,1,0:T(4,128)S(1)} %get-tuple-element.11), channel_id=1, source_target_pairs={{16,0},{32,16},{48,32},{64,48},{80,64},{96,80},{112,96},{128,112},... | collective-permute-start | bytes 175112 | tf_op jit(solution)/shard_map/ppermute | solution.py:18
  105.6 6.5 %copy-start.3 = (bf16[38,608]{1,0:T(8,128)(2,1)S(1)}, bf16[38,608]{1,0:T(8,128)(2,1)}, u32[]{:S(2)}) copy-start(bf16[38,608]{1,0:T(8,128)(2,1)} %param.15) | copy-start | bytes 138628
  107.2 31.1 %all-to-all-start.1 = ((bf16[38,16,256]{2,0,1:T(8,128)(2,1)}), bf16[38,16,256]{2,0,1:T(8,128)(2,1)S(1)}, u32[]{:S(2)}, u32[]{:S(2)}) async-start(bf16[38,16,256]{2,0,1:T(8,128)(2,1)} %copy.13), calls=%async_computation.1 | async-start | bytes 655360 | tf_op jit(solution)/shard_map/all_to_all | solution.py:67
Sparse Core Ops, SparseCore 0:
  38.2 54.4 all-gather.3
